TPU v7x, 32 devices: a whole 2x2x4 slice. The times are simulated.
32 devices in a mesh: occ: 4 (over y, x), vir: 8 (over z, core).
Axes of the slice: x: 2, y: 2, z: 4, core: 2. Of those that a mesh axis runs over, the one named last changes fastest.
Arguments:
- amplitudes: bfloat16 [1504, 3072], P('occ', 'vir'), may hold values from -6 to 6
- integrals: bfloat16 [3072, 3072], P(None, 'vir'), may hold values from -0.15625 to 0.15625
- tile_block: int32 [24], replicated, may hold values from 0 to 5, as said below
- pair_mask: int32 [6, 6], replicated, may hold values 0 or 1
- partner: int32 [1504], P('occ'), may hold values from 0 to 1503, as said below
Outputs:
- residual: float32 [1504, 3072], P('occ', 'vir')
Inputs may be any that keep to these rules, and one draw needn't show every extreme that they name: partner is an involution without fixed points: partner[partner[r]] = r and partner[r] != r. tile_block never falls along the tiles, and each of the 6 blocks holds at least one tile.
All inputs are finite; a program needn't handle non-finite values.
Results may differ from a plain program's by a relative error of at most 0.0003.
Values may be sent and summed in bfloat16 or wider, within the bound.
No kernel may reach another device: no remote copies, remote signals or barrier semaphores. Data moves between devices by JAX's collectives and lax.ppermute only.
A program may use at most 128 MiB of HBM per device.

v0:
```python
import jax
import jax.numpy as jnp
from jax import lax
from jax.sharding import PartitionSpec as P

TILE = 128


def body(amplitudes, integrals, tile_block, pair_mask, partner):
    columns = integrals.shape[1]
    local_tiles = columns // TILE
    total_tiles = tile_block.shape[0]
    groups = pair_mask.shape[0]
    first_tile = lax.axis_index("vir") * local_tiles
    own_blocks = lax.dynamic_slice_in_dim(tile_block, first_tile, local_tiles)
    labels = jnp.arange(groups, dtype=jnp.int32)
    row_onehot = (tile_block[:, None] == labels[None, :]).astype(jnp.float32)
    col_onehot = (own_blocks[:, None] == labels[None, :]).astype(jnp.float32)
    live_tiles = jnp.dot(jnp.dot(row_onehot, pair_mask.astype(jnp.float32)), col_onehot.T)
    masked = (
        integrals.reshape(total_tiles, TILE, local_tiles, TILE)
        * live_tiles.astype(jnp.bfloat16)[:, None, :, None]
    )
    masked = masked.reshape(integrals.shape)
    own_count = amplitudes.shape[0]
    gathered = lax.all_gather(amplitudes, "occ", axis=0, tiled=True)
    partner_rows = jnp.take(gathered, partner, axis=0)
    stacked = jnp.concatenate((amplitudes, partner_rows), axis=0)
    pair_sums = jnp.dot(
        lax.all_gather(stacked, "vir", axis=1, tiled=True),
        masked,
        preferred_element_type=jnp.float32,
    )
    residual = pair_sums[:own_count] - pair_sums[own_count:]
    return residual


def solution(mesh):
    placed = (P("occ", "vir"), P(None, "vir"), P(), P(), P("occ"))
    return jax.shard_map(
        body, mesh=mesh, in_specs=placed, out_specs=P("occ", "vir"), check_vma=False
    )
```

profile of v0, /device:TPU:0, one launch (start us, length us, event | category | flops | bytes accessed | tf_op | source)
XLA Modules:
  0.0 107.5 jit_solution(9422348159117418414)
XLA Ops:
  6.5 0.0 copy-start.2
  6.5 0.0 all-gather.3.cloned.1.call-start
  6.5 0.7 all-gather.3.cloned.1.call-update
  7.3 0.0 all-gather.5.cloned.1.call-start
  7.3 0.7 compare_select_fusion
  8.0 0.7 compare_and_fusion
  8.7 0.0 copy-start
  8.7 30.6 %all-gather.3.cloned.1.call-done = bf16[1504,384]{1,0:T(8,128)(2,1)} async-done(((bf16[376,384]{1,0:T(8,128)(2,1)}), bf16[1504,384]{1,0:T(8,128)(2,1)}) %all-gather.3.cloned.1.call-update) | async-done | bytes 1155088 | tf_op jit(solution)/shard_map/all_gather | solution.py:26
  39.3 3.4 %gather_fusion = bf16[376,384]{1,0:T(8,128)(2,1)S(1)} fusion(bf16[1504,384]{1,0:T(8,128)(2,1)} %all-gather.3.cloned.1.call-done, s32[1024]{0:T(1024)S(1)} %pad_clamp_fusion), kind=kCustom, calls=%fused_computation | custom fusion | bytes 579040 | tf_op jit(solution)/shard_map/jit(_take)/gather | solution.py:27
  42.7 0.1 broadcast_select_fusion
  42.9 0.0 copy-done.2
  42.9 0.9 pad_maximum_fusion
  43.7 0.0 all-gather.5.cloned.1.call-update
  43.8 0.0 copy-done
  43.8 0.0 copy-start.4
  43.8 0.0 copy-start.3
  43.8 2.6 %copy.7 = bf16[3072,384]{0,1:T(8,128)(2,1)} copy(bf16[3072,384]{1,0:T(8,128)(2,1)S(1)} %copy-done) | data formatting | bytes 4718592 | tf_op args[1]
  46.4 0.0 copy-start.1
  46.4 0.0 copy-done.4
  46.4 0.1 dynamic_slice.3
  46.5 0.0 copy-done.3
  46.5 0.3 fusion.5
  46.8 47.7 %all-gather.5.cloned.1.call-done = bf16[752,3072]{1,0:T(8,128)(2,1)} async-done(((bf16[752,384]{1,0:T(8,128)(2,1)}), bf16[752,3072]{1,0:T(8,128)(2,1)}) %all-gather.5.cloned.1.call-update) | async-done | bytes 4620304 | tf_op jit(solution)/shard_map/all_gather | solution.py:30
  94.5 0.4 mul.15
  94.9 0.0 copy-done.1
  94.9 4.9 %fusion = f32[752,384]{1,0:T(8,128)S(1)} fusion(bf16[752,3072]{1,0:T(8,128)(2,1)} %all-gather.5.cloned.1.call-done, bf16[3072,384]{0,1:T(8,128)(2,1)S(1)} %copy-done.1, bf16[48,8,24,128]{3,2,1,0:T(8,128)(2,1)S(1)} %bitcast.8), kind=kOutput, calls=%fused_computation.2 | convolution fusion | flops 1775370240 | bytes 10493952 | tf_op jit(solution)/shard_map/dot_general | solution.py:29
  99.8 0.9 slice_subtract_fusion
  (1 shorter events, 0.0 us)
Async XLA Ops:
  6.5 36.3 %copy-start.2 = (bf16[376,384]{1,0:T(8,128)(2,1)S(1)}, bf16[376,384]{1,0:T(8,128)(2,1)}, u32[]{:S(2)}) copy-start(bf16[376,384]{1,0:T(8,128)(2,1)} %param.5) | copy-start | bytes 866308
  6.5 32.8 %all-gather.3.cloned.1.call-start = ((), (), s32[]{:S(2)}) async-start(), calls=%async_computation | async-start | bytes 1443840 | tf_op jit(solution)/shard_map/all_gather | solution.py:26
  7.3 87.3 %all-gather.5.cloned.1.call-start = ((), (), s32[]{:S(2)}) async-start(), calls=%async_computation.1 | async-start | bytes 5197824 | tf_op jit(solution)/shard_map/all_gather | solution.py:30
  8.7 35.1 %copy-start = (bf16[3072,384]{1,0:T(8,128)(2,1)S(1)}, bf16[3072,384]{1,0:T(8,128)(2,1)}, u32[]{:S(2)}) copy-start(bf16[3072,384]{1,0:T(8,128)(2,1)} %param.6) | copy-start | bytes 7077892
  43.8 2.7 %copy-start.4 = (s32[24]{0:T(128)S(1)}, s32[24]{0:T(128)}, u32[]{:S(2)}) copy-start(s32[24]{0:T(128)} %param.7) | copy-start | bytes 292
  43.8 2.7 %copy-start.3 = (s32[6,6]{1,0:T(8,128)S(1)}, s32[6,6]{1,0:T(8,128)}, u32[]{:S(2)}) copy-start(s32[6,6]{1,0:T(8,128)} %param.8) | copy-start | bytes 436
  46.4 48.5 %copy-start.1 = (bf16[3072,384]{0,1:T(8,128)(2,1)S(1)}, bf16[3072,384]{0,1:T(8,128)(2,1)}, u32[]{:S(2)}) copy-start(bf16[3072,384]{0,1:T(8,128)(2,1)} %copy.7) | copy-start | bytes 7077892
Sparse Core Ops, SparseCore 0:
  9.2 30.0 all-gather.2
  43.9 50.6 all-gather.4
where the time goes:
time: 108 us
  waiting for transfers between devices  79.1 us (73%)
  between operations  13.5 us (12%)
  local copies, waits for them, and re-layouts  6.49 us (6%)
  matrix products  5.19 us (5%)
  other arithmetic  3.24 us (3%)
    all_gather x1, waiting for transfers between devices, body(): lax.all_gather(stacked, 'vir', axis=1, tiled=True)  47.7 us
    all_gather x1, waiting for transfers between devices, body(): gathered = lax.all_gather(amplitudes, 'occ', axis=0, tiled=True)  30.6 us
    dot_general x1, matrix products, body(): jnp.dot(lax.all_gather(stacked, 'vir', axis=1, tiled=True), masked, prefe...  4.88 us
    gather x1, local copies, waits for them, and re-layouts, body(): partner_rows = jnp.take(gathered, partner, axis=0)  3.4 us
    unnamed x11, local copies, waits for them, and re-layouts  2.65 us
  transfers between devices with their start and end apart: 2, of which 2 were waited for; matrix products, arithmetic and copies ran while one was open for 4% of the time, Pallas kernels for 0%

commit v1 on v0

--- a/solution.py
+++ b/solution.py
@@ -23,7 +23,12 @@
     )
     masked = masked.reshape(integrals.shape)
     own_count = amplitudes.shape[0]
-    gathered = lax.all_gather(amplitudes, "occ", axis=0, tiled=True)
+    ring = [amplitudes]
+    for hop in range(3):
+        ring.append(lax.ppermute(ring[-1], "occ", [(dev, (dev + 1) % 4) for dev in range(4)]))
+    gathered = jnp.roll(
+        jnp.concatenate(ring[::-1], axis=0), (lax.axis_index("occ") + 1) * ring[0].shape[0], axis=0
+    )
     partner_rows = jnp.take(gathered, partner, axis=0)
     stacked = jnp.concatenate((amplitudes, partner_rows), axis=0)
     pair_sums = jnp.dot(

time: 108 us -> 103 us (0.954)
  waiting for transfers between devices: 79.1 us -> 70.4 us
  starting transfers between devices: 0.04 us -> 3.69 us
    all_gather x1 -> x0, waiting for transfers between devices: 30.6 us -> none  [body(): gathered = lax.all_gather(amplitudes, 'occ', axis=0, tiled=True)]
    ppermute x0 -> x3, waiting for transfers between devices: none -> 23 us  [body(): lax.ppermute(ring[-1], 'occ', [(dev, (dev + 1) % 4) for dev in range(4)])]
    ppermute x0 -> x3, starting transfers between devices: none -> 3.69 us  [body(): lax.ppermute(ring[-1], 'occ', [(dev, (dev + 1) % 4) for dev in range(4)])]
    unnamed x11 -> x14, local copies, waits for them, and re-layouts: 2.65 us -> 4.14 us
    gather x1, local copies, waits for them, and re-layouts: 3.4 us -> 2.12 us  [body(): partner_rows = jnp.take(gathered, partner, axis=0)]
  transfers between devices with their start and end apart: 2 -> 4, of which waited for: 2 -> 4; matrix products, arithmetic and copies ran while one was open for 4% -> 4% of each run, Pallas kernels for 0% -> 0%
where the time goes in v1:
time: 103 us
  waiting for transfers between devices  70.4 us (68%)
  between operations  13.5 us (13%)
  local copies, waits for them, and re-layouts  7.06 us (7%)
  matrix products  5.19 us (5%)
  starting transfers between devices  3.69 us (4%)
  other arithmetic  3.24 us (3%)
    all_gather x1, waiting for transfers between devices, body(): lax.all_gather(stacked, 'vir', axis=1, tiled=True)  47.4 us
    ppermute x3, waiting for transfers between devices, body(): lax.ppermute(ring[-1], 'occ', [(dev, (dev + 1) % 4) for dev in range(4)])  23 us
    dot_general x1, matrix products, body(): jnp.dot(lax.all_gather(stacked, 'vir', axis=1, tiled=True), masked, prefe...  4.88 us
    unnamed x14, local copies, waits for them, and re-layouts  4.14 us
    ppermute x3, starting transfers between devices, body(): lax.ppermute(ring[-1], 'occ', [(dev, (dev + 1) % 4) for dev in range(4)])  3.69 us
    gather x1, local copies, waits for them, and re-layouts, body(): partner_rows = jnp.take(gathered, partner, axis=0)  2.12 us
  transfers between devices with their start and end apart: 4, of which 4 were waited for; matrix products, arithmetic and copies ran while one was open for 4% of the time, Pallas kernels for 0%

profile of v1, /device:TPU:0, one launch (start us, length us, event | category | flops | bytes accessed | tf_op | source)
XLA Modules:
  0.0 103.1 jit_solution(14525994498825459020)
XLA Ops:
  6.5 0.0 copy-start
  6.5 0.0 all-gather.2.cloned.1.call-start
  6.5 3.0 %collective-permute-start = (bf16[376,384]{1,0:T(8,128)(2,1)}, bf16[376,384]{1,0:T(8,128)(2,1)S(1)}, u32[]{:S(2)}, u32[]{:S(2)}) collective-permute-start(bf16[376,384]{1,0:T(8,128)(2,1)} %param.5), channel_id=1, source_target_pairs={{0,8},{8,16},{16,24},{24,0},{1,9},{9,17},{17,25},{25,1},{2,10},{10... | collective-permute-start | bytes 866312 | tf_op jit(solution)/shard_map/ppermute | solution.py:28
  9.5 8.1 %collective-permute-done = bf16[376,384]{1,0:T(8,128)(2,1)S(1)} collective-permute-done((bf16[376,384]{1,0:T(8,128)(2,1)}, bf16[376,384]{1,0:T(8,128)(2,1)S(1)}, u32[]{:S(2)}, u32[]{:S(2)}) %collective-permute-start) | collective-permute-done | bytes 288800 | tf_op jit(solution)/shard_map/ppermute | solution.py:28
  17.6 0.7 collective-permute-start.1
  18.3 0.7 compare_select_fusion
  19.0 7.5 %collective-permute-done.1 = bf16[376,384]{1,0:T(8,128)(2,1)S(1)} collective-permute-done((bf16[376,384]{1,0:T(8,128)(2,1)S(1)}, bf16[376,384]{1,0:T(8,128)(2,1)S(1)}, u32[]{:S(2)}, u32[]{:S(2)}) %collective-permute-start.1) | collective-permute-done | bytes 288800 | tf_op jit(solution)/shard_map/ppermute | solution.py:28
  26.6 0.0 collective-permute-start.2
  26.6 0.7 compare_and_fusion
  27.3 7.4 %collective-permute-done.2 = bf16[376,384]{1,0:T(8,128)(2,1)S(1)} collective-permute-done((bf16[376,384]{1,0:T(8,128)(2,1)S(1)}, bf16[376,384]{1,0:T(8,128)(2,1)S(1)}, u32[]{:S(2)}, u32[]{:S(2)}) %collective-permute-start.2) | collective-permute-done | bytes 288800 | tf_op jit(solution)/shard_map/ppermute | solution.py:28
  34.8 1.0 constant_dynamic-update-slice_fusion.4
  36.0 0.0 copy-done
  36.0 0.3 constant_dynamic-slice_fusion
  36.3 2.1 %gather_fusion = bf16[376,384]{1,0:T(8,128)(2,1)S(1)} fusion(bf16[1504,384]{1,0:T(8,128)(2,1)S(1)} %constant_dynamic-slice_fusion, s32[1024]{0:T(1024)S(1)} %pad_clamp_fusion), kind=kCustom, calls=%fused_computation | custom fusion | bytes 579040 | tf_op jit(solution)/shard_map/jit(_take)/gather | solution.py:32
  38.5 0.1 broadcast_select_fusion
  38.6 0.9 pad_maximum_fusion
  39.5 0.0 all-gather.2.cloned.1.call-update
  39.5 0.0 copy-start.2
  39.5 0.0 copy-start.1
  39.5 2.8 %copy.7 = bf16[3072,384]{0,1:T(8,128)(2,1)S(1)} copy(bf16[3072,384]{1,0:T(8,128)(2,1)} %param.6) | data formatting | bytes 4718592 | tf_op args[1]
  42.4 0.0 copy-done.2
  42.4 0.1 dynamic_slice.8
  42.5 0.0 copy-done.1
  42.5 0.3 fusion.5
  42.8 47.4 %all-gather.2.cloned.1.call-done = bf16[752,3072]{1,0:T(8,128)(2,1)} async-done(((bf16[752,384]{1,0:T(8,128)(2,1)}), bf16[752,3072]{1,0:T(8,128)(2,1)}) %all-gather.2.cloned.1.call-update) | async-done | bytes 4620304 | tf_op jit(solution)/shard_map/all_gather | solution.py:35
  90.2 0.4 mul.19
  90.5 4.9 %fusion = f32[752,384]{1,0:T(8,128)S(1)} fusion(bf16[752,3072]{1,0:T(8,128)(2,1)} %all-gather.2.cloned.1.call-done, bf16[3072,384]{0,1:T(8,128)(2,1)S(1)} %copy.7, bf16[48,8,24,128]{3,2,1,0:T(8,128)(2,1)S(1)} %bitcast.8), kind=kOutput, calls=%fused_computation.2 | convolution fusion | flops 1775370240 | bytes 10493952 | tf_op jit(solution)/shard_map/dot_general | solution.py:34
  95.4 0.9 slice_subtract_fusion
  (8 shorter events, 0.3 us)
Async XLA Ops:
  6.5 29.4 %copy-start = (bf16[376,384]{1,0:T(8,128)(2,1)S(1)}, bf16[376,384]{1,0:T(8,128)(2,1)}, u32[]{:S(2)}) copy-start(bf16[376,384]{1,0:T(8,128)(2,1)} %param.5) | copy-start | bytes 866308
  6.5 83.6 %all-gather.2.cloned.1.call-start = ((), (), s32[]{:S(2)}) async-start(), calls=%async_computation | async-start | bytes 5197824 | tf_op jit(solution)/shard_map/all_gather | solution.py:35
  6.5 11.1 %collective-permute-start = (bf16[376,384]{1,0:T(8,128)(2,1)}, bf16[376,384]{1,0:T(8,128)(2,1)S(1)}, u32[]{:S(2)}, u32[]{:S(2)}) collective-permute-start(bf16[376,384]{1,0:T(8,128)(2,1)} %param.5), channel_id=1, source_target_pairs={{0,8},{8,16},{16,24},{24,0},{1,9},{9,17},{17,25},{25,1},{2,10},{10... | collective-permute-start | bytes 866312 | tf_op jit(solution)/shard_map/ppermute | solution.py:28
  17.6 8.9 %collective-permute-start.1 = (bf16[376,384]{1,0:T(8,128)(2,1)S(1)}, bf16[376,384]{1,0:T(8,128)(2,1)S(1)}, u32[]{:S(2)}, u32[]{:S(2)}) collective-permute-start(bf16[376,384]{1,0:T(8,128)(2,1)S(1)} %collective-permute-done), channel_id=1, source_target_pairs={{0,8},{8,16},{16,24},{24,0},{1,9},{9,17},{17,25},{25,1},{2,10},{10... | collective-permute-start | bytes 866312 | tf_op jit(solution)/shard_map/ppermute | solution.py:28
  26.6 8.1 %collective-permute-start.2 = (bf16[376,384]{1,0:T(8,128)(2,1)S(1)}, bf16[376,384]{1,0:T(8,128)(2,1)S(1)}, u32[]{:S(2)}, u32[]{:S(2)}) collective-permute-start(bf16[376,384]{1,0:T(8,128)(2,1)S(1)} %collective-permute-done.1), channel_id=1, source_target_pairs={{0,8},{8,16},{16,24},{24,0},{1,9},{9,17},{17,25},{25,1},{2,10},{10... | collective-permute-start | bytes 866312 | tf_op jit(solution)/shard_map/ppermute | solution.py:28
  39.5 2.9 %copy-start.2 = (s32[24]{0:T(128)S(1)}, s32[24]{0:T(128)}, u32[]{:S(2)}) copy-start(s32[24]{0:T(128)} %param.7) | copy-start | bytes 292
  39.5 3.0 %copy-start.1 = (s32[6,6]{1,0:T(8,128)S(1)}, s32[6,6]{1,0:T(8,128)}, u32[]{:S(2)}) copy-start(s32[6,6]{1,0:T(8,128)} %param.8) | copy-start | bytes 436
Sparse Core Ops, SparseCore 0:
  39.6 50.5 all-gather.1
